TPU v7x, 32 devices: a whole 2x2x4 slice. The times are simulated.
32 devices in a mesh: dom: 2 (over y), loop: 4 (over z), trip: 2 (over x), rep: 2 (over core).
Axes of the slice: x: 2, y: 2, z: 4, core: 2. Of those that a mesh axis runs over, the one named last changes fastest.
Arguments:
- cubic_coupling_slices: bfloat16 [8, 120, 120], P(('dom', 'loop')), parts along dimension 0, may hold values from -6 to 6
- leading_displacement_label: int32 [8], P(('dom', 'loop')), parts along dimension 0, may hold values from 0 to 119
- lattice_shift_pairs: int32 [8, 6], P(('dom', 'loop')), parts along dimension 0, may hold values from 0 to 2
- polarization_vectors: bfloat16 [64, 2, 120, 120], P(('dom', 'trip')), parts along dimension 0, may hold values from -0.5 to 0.5
- mode_pulsations: bfloat16 [64, 120], P(('dom', 'trip')), parts along dimension 0, may hold values from 1 to 4
- momentum_slot_lookup: int32 [64], P('dom'), parts along dimension 0, may hold values from 0 to 31, as said below
- momentum_trios: int32 [64, 3], P(('dom', 'loop', 'trip')), parts along dimension 0, may hold values from 0 to 31, as said below
- thermal_label: int32 [64], P(('dom', 'loop', 'trip')), parts along dimension 0, may hold values from 0 to 7
Outputs:
- strength: float32 [64, 120], P(('dom', 'loop', 'trip'), 'rep'), parts along dimension 0
There are 2 independent parts, one for each index of `dom`. A program takes and returns all parts, laid end to end along the dimension named above; each array names one. Nothing has to cross between parts.
Inputs may be any that keep to these rules, and one draw needn't show every extreme that they name: `momentum_slot_lookup`: each number from 0 to 31 appears once: entry q is the location of q-point q's eigenvectors and frequencies. `momentum_trios`: in each aligned block of 4 rows (the triplets of one device), of the 12 named q-points (repeats counted) at most 12 have momentum_slot_lookup in one range [o * 16, (o + 1) * 16), and exactly 12 fall in some range.
All inputs are finite; a program needn't handle non-finite values.
Results may differ from a plain program's by a relative error of at most 0.00093.
Values may be sent and summed in bfloat16 or wider, within the bound.
A program may use at most 64 MiB of HBM per device.

v0:
```python
import math

import jax
import jax.numpy as jnp
from jax import lax
from jax.sharding import PartitionSpec as P

QGRID = 8


def passed_along(value, axis, steps):
    count = lax.axis_size(axis)
    pairs = [(source, (source + steps) % count) for source in range(count)]
    return lax.ppermute(value, axis, pairs)


def grid_coords(qpoint):
    return jnp.stack(
        [qpoint % QGRID, qpoint // QGRID % QGRID, qpoint // (QGRID * QGRID) % QGRID], axis=-1
    )


def per_device(
    cubic_coupling_slices,
    leading_displacement_label,
    lattice_shift_pairs,
    polarization_vectors,
    mode_pulsations,
    momentum_slot_lookup,
    momentum_trios,
    thermal_label,
):
    rows_dev = cubic_coupling_slices.shape[0]
    width = cubic_coupling_slices.shape[1]
    trip_dev = momentum_trios.shape[0]
    loop_size = lax.axis_size("loop")
    trip_size = lax.axis_size("trip")
    columns = width // lax.axis_size("rep")
    total_rows = rows_dev * loop_size
    q_held = polarization_vectors.shape[0]
    wanted = momentum_trios.reshape(-1)
    wanted_count = wanted.shape[0]
    catalog = jnp.arange(momentum_slot_lookup.shape[0], dtype=jnp.int32)
    located = jnp.sum(
        jnp.where(wanted[:, None] == catalog[None, :], momentum_slot_lookup[None, :], 0), axis=1
    )
    capacity = 2 * wanted_count // trip_size
    holders = located // q_held
    slots = located % q_held
    ranking = jnp.arange(wanted_count, dtype=jnp.int32)
    earlier = (holders[:, None] == holders[None, :]) & (ranking[None, :] < ranking[:, None])
    position = jnp.sum(earlier.astype(jnp.int32), axis=1)
    matched = (holders[None, None, :] == jnp.arange(trip_size, dtype=jnp.int32)[:, None, None]) & (
        position[None, None, :] == jnp.arange(capacity, dtype=jnp.int32)[None, :, None]
    )
    asking = jnp.sum(jnp.where(matched, slots[None, None, :] + 1, 0), axis=2) - 1
    received = lax.all_to_all(asking, "trip", split_axis=0, concat_axis=0, tiled=True)
    usable = received >= 0
    chosen = jnp.clip(received, 0, q_held - 1)
    sent_blocks = jnp.where(
        usable[:, :, None, None, None],
        polarization_vectors[chosen],
        jnp.zeros((), polarization_vectors.dtype),
    )
    sent_levels = jnp.where(
        usable[:, :, None], mode_pulsations[chosen], jnp.zeros((), mode_pulsations.dtype)
    )
    got_blocks = lax.all_to_all(sent_blocks, "trip", split_axis=0, concat_axis=0, tiled=True)
    got_levels = lax.all_to_all(sent_levels, "trip", split_axis=0, concat_axis=0, tiled=True)
    flat_index = holders * capacity + position
    blocks = got_blocks.reshape((trip_size * capacity,) + got_blocks.shape[2:])[flat_index]
    levels = got_levels.reshape(trip_size * capacity, width)[flat_index]
    blocks = blocks.reshape(trip_dev, 3, 2, width, width)
    levels = levels.reshape(trip_dev, 3, width).astype(jnp.float32)
    first_vec = blocks[:, 0]
    second_vec = blocks[:, 1]
    rep_start = lax.axis_index("rep") * columns
    third_part = lax.dynamic_slice_in_dim(blocks[:, 2], rep_start, columns, 3)
    closing_energy = lax.dynamic_slice_in_dim(levels[:, 2], rep_start, columns, 1)
    right_side = third_part.transpose(2, 0, 1, 3).reshape(width, trip_dev * 2 * columns)
    second_re = jnp.swapaxes(second_vec[:, 0], 1, 2)
    second_im = jnp.swapaxes(second_vec[:, 1], 1, 2)
    mixer = jnp.concatenate(
        [
            jnp.concatenate([second_re, -second_im], axis=2),
            jnp.concatenate([second_im, second_re], axis=2),
        ],
        axis=1,
    )
    second_grid = grid_coords(momentum_trios[:, 1])
    third_grid = grid_coords(momentum_trios[:, 2])
    first_re = first_vec[:, 0]
    first_im = first_vec[:, 1]

    def absorb(force_slab, slab_modes, slab_cells, first_row, stacks):
        mixed_all, coeff_all = stacks
        count = force_slab.shape[0]
        hidden = jnp.dot(
            force_slab.reshape(count * width, width), right_side, preferred_element_type=jnp.float32
        ).astype(jnp.bfloat16)
        hidden = (
            hidden.reshape(count, width, trip_dev, 2, columns)
            .transpose(2, 0, 3, 1, 4)
            .reshape(trip_dev, count, 2 * width, columns)
        )
        mixed = jnp.einsum(
            "tab,tsbk->tsak", mixer, hidden, preferred_element_type=jnp.float32
        ).astype(jnp.bfloat16)
        mixed = mixed.reshape(trip_dev, count * 2, width * columns)
        offsets = slab_cells - 1
        turns = jnp.sum(second_grid[:, None, :] * offsets[None, :, :3], axis=2) + jnp.sum(
            third_grid[:, None, :] * offsets[None, :, 3:], axis=2
        )
        angle = 2.0 * math.pi / QGRID * jnp.mod(turns, QGRID).astype(jnp.float32)
        cosine = jnp.cos(angle)[:, :, None]
        sine = jnp.sin(angle)[:, :, None]
        picked_re = first_re[:, slab_modes, :].astype(jnp.float32)
        picked_im = first_im[:, slab_modes, :].astype(jnp.float32)
        coef_re = jnp.swapaxes((picked_re * cosine - picked_im * sine).astype(jnp.bfloat16), 1, 2)
        coef_im = jnp.swapaxes((picked_re * sine + picked_im * cosine).astype(jnp.bfloat16), 1, 2)
        coeff = jnp.stack(
            [jnp.stack([coef_re, -coef_im], axis=-1), jnp.stack([coef_im, coef_re], axis=-1)],
            axis=1,
        ).reshape(trip_dev, 2 * width, count * 2)
        row_start = first_row * 2
        mixed_all = lax.dynamic_update_slice_in_dim(mixed_all, mixed, row_start, 1)
        coeff_all = lax.dynamic_update_slice_in_dim(coeff_all, coeff, row_start, 2)
        return (mixed_all, coeff_all)

    stacks = (
        jnp.zeros((trip_dev, total_rows * 2, width * columns), jnp.bfloat16),
        jnp.zeros((trip_dev, 2 * width, total_rows * 2), jnp.bfloat16),
    )
    stacks = absorb(
        cubic_coupling_slices, leading_displacement_label, lattice_shift_pairs, 0, stacks
    )

    def advance_both(stop, carried):
        upward, downward, held = carried
        upward = passed_along((upward[0], upward[1], upward[2]), "loop", 1)
        downward = passed_along((downward[0], downward[1], downward[2]), "loop", -1)
        held = absorb(upward[0], upward[1], upward[2], (2 * stop - 1) * rows_dev, held)
        held = absorb(downward[0], downward[1], downward[2], 2 * stop * rows_dev, held)
        return (upward, downward, held)

    starting = (cubic_coupling_slices, leading_displacement_label, lattice_shift_pairs)
    upward, downward, stacks = lax.fori_loop(
        1, loop_size // 2, advance_both, (starting, starting, stacks)
    )
    upward = passed_along((upward[0], upward[1], upward[2]), "loop", 1)
    stacks = absorb(upward[0], upward[1], upward[2], (loop_size - 1) * rows_dev, stacks)
    thermal_kelvin_list = 0.5 * (thermal_label.astype(jnp.float32) + 1.0)
    partner_energy = levels[:, 1]
    partner_population = 1.0 / jnp.expm1(partner_energy / thermal_kelvin_list[:, None])
    closing_population = 1.0 / jnp.expm1(closing_energy / thermal_kelvin_list[:, None])
    weights = (
        (1.0 + partner_population[:, :, None] + closing_population[:, None, :])
        / (partner_energy[:, :, None] * closing_energy[:, None, :])
    ).reshape(trip_dev, width * columns)

    def finish(items):
        mixed_one, coeff_one, weight_one = items
        amplitude = jnp.dot(coeff_one, mixed_one, preferred_element_type=jnp.float32)
        power = amplitude[:width] ** 2 + amplitude[width:] ** 2
        return jnp.dot(power, weight_one, precision=lax.Precision.HIGHEST)

    partial_sums = lax.map(finish, (stacks[0], stacks[1], weights))
    partial_sums = partial_sums * (1.0 / (8.0 * width * total_rows)) / levels[:, 0]
    return lax.psum_scatter(partial_sums, "rep", scatter_dimension=1, tiled=True)


def solution(mesh):
    in_specs = (
        P(("dom", "loop"), None, None),
        P(("dom", "loop")),
        P(("dom", "loop"), None),
        P(("dom", "trip"), None, None, None),
        P(("dom", "trip"), None),
        P("dom"),
        P(("dom", "loop", "trip"), None),
        P(("dom", "loop", "trip")),
    )
    out_specs = P(("dom", "loop", "trip"), "rep")
    return jax.shard_map(
        per_device, mesh=mesh, in_specs=in_specs, out_specs=out_specs, check_vma=False
    )
```

profile of v0, /device:TPU:0, one launch (start us, length us, event | category | flops | bytes accessed | tf_op | source)
XLA Modules:
  0.0 96.1 jit_solution(14769082474178184088)
XLA Ops:
  0.0 3.1 %collective-permute-start.6 = (bf16[1,120,120]{2,1,0:T(8,128)(2,1)}, bf16[1,120,120]{2,1,0:T(8,128)(2,1)S(1)}, u32[]{:S(2)}, u32[]{:S(2)}) collective-permute-start(bf16[1,120,120]{2,1,0:T(8,128)(2,1)} %param.10), channel_id=1, source_target_pairs={{0,4},{4,8},{8,12},{12,0},{1,5},{5,9},{9,13},{13,1},{2,6},{6,10},{... | collective-permute-start | bytes 86408 | tf_op jit(solution)/shard_map/while/body/eval_jaxpr/ppermute | solution.py:14
  3.1 2.1 %collective-permute-start.7 = (bf16[1,120,120]{2,1,0:T(8,128)(2,1)}, bf16[1,120,120]{2,1,0:T(8,128)(2,1)S(1)}, u32[]{:S(2)}, u32[]{:S(2)}) collective-permute-start(bf16[1,120,120]{2,1,0:T(8,128)(2,1)} %param.10), channel_id=1, source_target_pairs={{0,12},{4,0},{8,4},{12,8},{1,13},{5,1},{9,5},{13,9},{2,14},{6,2},{... | collective-permute-start | bytes 86408 | tf_op jit(solution)/shard_map/while/body/eval_jaxpr/ppermute | solution.py:14
  5.1 3.8 %collective-permute-start.3 = (s32[1,6]{1,0:T(1,128)}, s32[1,6]{1,0:T(1,128)S(1)}, u32[]{:S(2)}, u32[]{:S(2)}) collective-permute-start(s32[1,6]{1,0:T(1,128)} %param.12), channel_id=1, source_target_pairs={{0,12},{4,0},{8,4},{12,8},{1,13},{5,1},{9,5},{13,9},{2,14},{6,2},{... | collective-permute-start | bytes 80 | tf_op jit(solution)/shard_map/while/body/eval_jaxpr/ppermute | solution.py:14
  9.0 0.8 eq.79
  9.7 0.8 select_reduce_fusion
  10.8 0.3 fusion.24
  11.1 0.6 copy.173
  11.7 3.2 %all-to-all-start = ((s32[2,1,12]{2,1,0:T(1,128)}), s32[2,1,12]{2,1,0:T(1,128)S(1)}, u32[]{:S(2)}, u32[]{:S(2)}) async-start(s32[2,1,12]{2,1,0:T(1,128)} %bitcast.4), calls=%async_computation | async-start | bytes 2048 | tf_op jit(solution)/shard_map/all_to_all | solution.py:57
  15.0 0.8 sign_compare_fusion.1
  15.9 0.7 broadcast_add_fusion.4
  17.3 0.7 add_multiply_fusion
  17.9 1.2 %dynamic-slice.42 = u32[1]{0:T(128)} dynamic-slice(u32[32]{0:T(128)} %constant.386, u32[]{:T(128)S(6)} %add.434), dynamic_slice_sizes={1} | dynamic-slice | bytes 12
  19.7 1.0 %fusion.50 = (s32[4]{0:T(128)S(1)}, s32[4]{0:T(128)S(1)}, s32[4]{0:T(128)S(1)}, s32[4]{0:T(128)S(1)}, s32[4]{0:T(128)S(1)}, /*index=5*/s32[4]{0:T(128)S(1)}) fusion(pred[4,1]{1,0:T(4,128)(4,1)S(1)} %get-tuple-element.234, pred[4,1]{1,0:T(4,128)(4,1)S(1)} %get-tuple-element.233, s32[4,3]{1,0:T(4,128)} %param.16, pred[4,1]{1,0:T(4,128)(4,1)S(1)} %get-tuple-element.235, ...), kind=kLoop, calls=%fused_computation.149 | loop fusion | flops 384 | bytes 144 | tf_op jit(solution)/shard_map/jit(remainder)/select_n | solution.py:19
  20.8 3.9 %collective-permute-start.2 = (s32[1]{0:T(128)}, s32[1]{0:T(128)}, u32[]{:S(2)}, u32[]{:S(2)}) collective-permute-start(s32[1]{0:T(128)} %param.11), channel_id=1, source_target_pairs={{0,12},{4,0},{8,4},{12,8},{1,13},{5,1},{9,5},{13,9},{2,14},{6,2},{... | collective-permute-start | bytes 20 | tf_op jit(solution)/shard_map/while/body/eval_jaxpr/ppermute | solution.py:14
  28.7 3.3 %collective-permute-done.4 = s32[1]{0:T(128)} collective-permute-done((s32[1]{0:T(128)}, s32[1]{0:T(128)}, u32[]{:S(2)}, u32[]{:S(2)}) %collective-permute-start.4) | collective-permute-done | bytes 36 | tf_op jit(solution)/shard_map/ppermute | solution.py:14
  34.0 5.2 %collective-permute-done.5 = s32[1,6]{1,0:T(1,128)S(1)} collective-permute-done((s32[1,6]{1,0:T(1,128)S(1)}, s32[1,6]{1,0:T(1,128)S(1)}, u32[]{:S(2)}, u32[]{:S(2)}) %collective-permute-start.5) | collective-permute-done | bytes 56 | tf_op jit(solution)/shard_map/ppermute | solution.py:14
  39.3 0.8 gather_fusion
  40.1 1.3 %gather_fusion.2 = bf16[24,120]{1,0:T(8,128)(2,1)S(1)} fusion(bf16[16,120]{1,0:T(8,128)(2,1)} %param.14, s32[1024]{0:T(1024)S(1)} %pad_clamp_fusion.1), kind=kCustom, calls=%fused_computation.2 | custom fusion | bytes 11616 | tf_op jit(solution)/shard_map/gather | solution.py:66
  41.4 1.3 %broadcast_select_fusion = bf16[2,12,2,120,120]{4,3,2,1,0:T(8,128)(2,1)} fusion(bf16[2,12,2,120,120]{4,3,2,1,0:T(8,128)(2,1)S(1)} %bitcast.249, pred[2,12]{1,0:T(4,128)(4,1)S(1)} %bitcast.269), kind=kLoop, calls=%fused_computation.17 | loop fusion | flops 691200 | bytes 2764824 | tf_op jit(solution)/shard_map/jit(_where)/select_n | solution.py:60
  42.7 0.7 broadcast_select_fusion.1
  43.3 3.2 %all-to-all-start.2 = ((bf16[2,12,120]{2,1,0:T(8,128)(2,1)}), bf16[2,12,120]{2,1,0:T(8,128)(2,1)S(1)}, u32[]{:S(2)}, u32[]{:S(2)}) async-start(bf16[2,12,120]{2,1,0:T(8,128)(2,1)} %broadcast_select_fusion.1), calls=%async_computation.2 | async-start | bytes 16384 | tf_op jit(solution)/shard_map/all_to_all | solution.py:69
  47.1 3.3 %all-to-all-done.2 = bf16[2,12,120]{2,1,0:T(8,128)(2,1)S(1)} async-done(((bf16[2,12,120]{2,1,0:T(8,128)(2,1)}), bf16[2,12,120]{2,1,0:T(8,128)(2,1)S(1)}, u32[]{:S(2)}, u32[]{:S(2)}) %all-to-all-start.2) | async-done | bytes 5792 | tf_op jit(solution)/shard_map/all_to_all | solution.py:69
  50.4 3.7 %all-to-all-start.1 = ((bf16[2,12,2,120,120]{4,3,2,1,0:T(8,128)(2,1)}), bf16[2,12,2,120,120]{4,3,2,1,0:T(8,128)(2,1)S(1)}, u32[]{:S(2)}, u32[]{:S(2)}) async-start(bf16[2,12,2,120,120]{4,3,2,1,0:T(8,128)(2,1)} %broadcast_select_fusion), calls=%async_computation.1 | async-start | bytes 2949120 | tf_op jit(solution)/shard_map/all_to_all | solution.py:68
  54.1 0.6 gather_fusion.3
  54.9 0.2 multiply_divide_fusion
  55.2 0.2 collective-permute-start.8
  55.5 11.8 %all-to-all-done.1 = bf16[2,12,2,120,120]{4,3,2,1,0:T(8,128)(2,1)S(1)} async-done(((bf16[2,12,2,120,120]{4,3,2,1,0:T(8,128)(2,1)}), bf16[2,12,2,120,120]{4,3,2,1,0:T(8,128)(2,1)S(1)}, u32[]{:S(2)}, u32[]{:S(2)}) %all-to-all-start.1) | async-done | bytes 1382432 | tf_op jit(solution)/shard_map/all_to_all | solution.py:68
  67.3 0.7 gather_fusion.1
  70.3 0.4 fusion.13
  70.7 0.4 fusion.12
  71.0 0.2 fusion.18
  71.6 0.4 fusion.14
  72.1 0.4 reshape.1944
  72.7 0.4 reshape.1940
  73.2 0.4 reshape.1948
  74.1 0.4 fusion.15
  74.7 0.4 reshape.1952
  76.2 16.8 %while.14 = (s32[]{:T(128)}, f32[4,120]{1,0:T(4,128)S(1)}, bf16[4,240,8]{1,2,0:T(8,128)(2,1)S(1)}, bf16[4,8,7200]{2,1,0:T(8,128)(2,1)S(1)}, f32[4,7200]{1,0:T(4,128)S(1)}, /*index=5*/s32[]{:T(128)}, s32[]{:T(128)}) while((s32[]{:T(128)}, f32[4,120]{1,0:T(4,128)S(1)}, bf16[4,240,8]{1,2,0:T(8,128)(2,1)S(1)}, ...), condition=%wide.region_12.13_spmd, body=%wide.region_11.12_spmd.sunk | while | flops 40608000 | bytes 14068725 | solution.py:167
  76.2 1.1 %fusion.110 = f32[240,7200]{1,0:T(8,128)S(1)} fusion(bf16[4,8,7200]{2,1,0:T(8,128)(2,1)S(1)} %get-tuple-element.314, s32[]{:T(128)} %get-tuple-element.304, bf16[4,240,8]{1,2,0:T(8,128)(2,1)S(1)} %get-tuple-element.313), kind=kOutput, calls=%fused_computation.8.clone.1 | convolution fusion | flops 27648000 | bytes 7033856 | tf_op jit(solution)/shard_map/while/body/eval_jaxpr/dot_general | solution.py:163
  77.4 3.0 %fusion.111 = f32[1,120]{1,0:T(1,128)S(1)} fusion(f32[240,7200]{1,0:T(8,128)S(1)} %fusion.110, f32[4,7200]{1,0:T(4,128)S(1)} %get-tuple-element.315, s32[]{:T(128)} %get-tuple-element.304), kind=kOutput, calls=%fused_computation.6.clone.1 | convolution fusion | flops 12960000 | bytes 7033828 | tf_op jit(solution)/shard_map/while/body/eval_jaxpr/dot_general | solution.py:165
  80.4 1.1 %fusion.110 = f32[240,7200]{1,0:T(8,128)S(1)} fusion(bf16[4,8,7200]{2,1,0:T(8,128)(2,1)S(1)} %get-tuple-element.314, s32[]{:T(128)} %get-tuple-element.304, bf16[4,240,8]{1,2,0:T(8,128)(2,1)S(1)} %get-tuple-element.313), kind=kOutput, calls=%fused_computation.8.clone.1 | convolution fusion | flops 27648000 | bytes 7033856 | tf_op jit(solution)/shard_map/while/body/eval_jaxpr/dot_general | solution.py:163
  81.6 3.0 %fusion.111 = f32[1,120]{1,0:T(1,128)S(1)} fusion(f32[240,7200]{1,0:T(8,128)S(1)} %fusion.110, f32[4,7200]{1,0:T(4,128)S(1)} %get-tuple-element.315, s32[]{:T(128)} %get-tuple-element.304), kind=kOutput, calls=%fused_computation.6.clone.1 | convolution fusion | flops 12960000 | bytes 7033828 | tf_op jit(solution)/shard_map/while/body/eval_jaxpr/dot_general | solution.py:165
  84.6 1.1 %fusion.110 = f32[240,7200]{1,0:T(8,128)S(1)} fusion(bf16[4,8,7200]{2,1,0:T(8,128)(2,1)S(1)} %get-tuple-element.314, s32[]{:T(128)} %get-tuple-element.304, bf16[4,240,8]{1,2,0:T(8,128)(2,1)S(1)} %get-tuple-element.313), kind=kOutput, calls=%fused_computation.8.clone.1 | convolution fusion | flops 27648000 | bytes 7033856 | tf_op jit(solution)/shard_map/while/body/eval_jaxpr/dot_general | solution.py:163
  85.7 3.0 %fusion.111 = f32[1,120]{1,0:T(1,128)S(1)} fusion(f32[240,7200]{1,0:T(8,128)S(1)} %fusion.110, f32[4,7200]{1,0:T(4,128)S(1)} %get-tuple-element.315, s32[]{:T(128)} %get-tuple-element.304), kind=kOutput, calls=%fused_computation.6.clone.1 | convolution fusion | flops 12960000 | bytes 7033828 | tf_op jit(solution)/shard_map/while/body/eval_jaxpr/dot_general | solution.py:165
  88.8 1.1 %fusion.110 = f32[240,7200]{1,0:T(8,128)S(1)} fusion(bf16[4,8,7200]{2,1,0:T(8,128)(2,1)S(1)} %get-tuple-element.314, s32[]{:T(128)} %get-tuple-element.304, bf16[4,240,8]{1,2,0:T(8,128)(2,1)S(1)} %get-tuple-element.313), kind=kOutput, calls=%fused_computation.8.clone.1 | convolution fusion | flops 27648000 | bytes 7033856 | tf_op jit(solution)/shard_map/while/body/eval_jaxpr/dot_general | solution.py:163
  89.9 3.0 %fusion.111 = f32[1,120]{1,0:T(1,128)S(1)} fusion(f32[240,7200]{1,0:T(8,128)S(1)} %fusion.110, f32[4,7200]{1,0:T(4,128)S(1)} %get-tuple-element.315, s32[]{:T(128)} %get-tuple-element.304), kind=kOutput, calls=%fused_computation.6.clone.1 | convolution fusion | flops 12960000 | bytes 7033828 | tf_op jit(solution)/shard_map/while/body/eval_jaxpr/dot_general | solution.py:165
  93.0 2.5 %all-reduce.2 = f32[4,120]{1,0:T(4,128)S(1)} all-reduce(f32[4,120]{1,0:T(4,128)S(1)} %multiply_divide_fusion.1), channel_id=2, replica_groups=mesh['dom'=2,'loop'=4,'trip'=2,'rep'=2] {'rep'}, use_global_device_ids=true, to_apply=%region_13.14.clone | all-reduce | flops 480 | bytes 3840
  95.5 0.7 constant_dynamic-slice_fusion.10
  (118 shorter events, 6.6 us)
Async XLA Ops:
  0.0 39.3 %copy-start = (bf16[16,2,120,120]{3,2,1,0:T(8,128)(2,1)S(1)}, bf16[16,2,120,120]{3,2,1,0:T(8,128)(2,1)}, u32[]{:S(2)}) copy-start(bf16[16,2,120,120]{3,2,1,0:T(8,128)(2,1)} %param.13) | copy-start | bytes 2764804
  0.0 55.2 %collective-permute-start.6 = (bf16[1,120,120]{2,1,0:T(8,128)(2,1)}, bf16[1,120,120]{2,1,0:T(8,128)(2,1)S(1)}, u32[]{:S(2)}, u32[]{:S(2)}) collective-permute-start(bf16[1,120,120]{2,1,0:T(8,128)(2,1)} %param.10), channel_id=1, source_target_pairs={{0,4},{4,8},{8,12},{12,0},{1,5},{5,9},{9,13},{13,1},{2,6},{6,10},{... | collective-permute-start | bytes 86408 | tf_op jit(solution)/shard_map/while/body/eval_jaxpr/ppermute | solution.py:14
  3.1 68.0 %collective-permute-start.7 = (bf16[1,120,120]{2,1,0:T(8,128)(2,1)}, bf16[1,120,120]{2,1,0:T(8,128)(2,1)S(1)}, u32[]{:S(2)}, u32[]{:S(2)}) collective-permute-start(bf16[1,120,120]{2,1,0:T(8,128)(2,1)} %param.10), channel_id=1, source_target_pairs={{0,12},{4,0},{8,4},{12,8},{1,13},{5,1},{9,5},{13,9},{2,14},{6,2},{... | collective-permute-start | bytes 86408 | tf_op jit(solution)/shard_map/while/body/eval_jaxpr/ppermute | solution.py:14
  5.1 28.5 %collective-permute-start.1 = (s32[1,6]{1,0:T(1,128)}, s32[1,6]{1,0:T(1,128)S(1)}, u32[]{:S(2)}, u32[]{:S(2)}) collective-permute-start(s32[1,6]{1,0:T(1,128)} %param.12), channel_id=1, source_target_pairs={{0,4},{4,8},{8,12},{12,0},{1,5},{5,9},{9,13},{13,1},{2,6},{6,10},{... | collective-permute-start | bytes 80 | tf_op jit(solution)/shard_map/while/body/eval_jaxpr/ppermute | solution.py:14
  5.1 28.6 %collective-permute-start.3 = (s32[1,6]{1,0:T(1,128)}, s32[1,6]{1,0:T(1,128)S(1)}, u32[]{:S(2)}, u32[]{:S(2)}) collective-permute-start(s32[1,6]{1,0:T(1,128)} %param.12), channel_id=1, source_target_pairs={{0,12},{4,0},{8,4},{12,8},{1,13},{5,1},{9,5},{13,9},{2,14},{6,2},{... | collective-permute-start | bytes 80 | tf_op jit(solution)/shard_map/while/body/eval_jaxpr/ppermute | solution.py:14
  11.7 22.1 %all-to-all-start = ((s32[2,1,12]{2,1,0:T(1,128)}), s32[2,1,12]{2,1,0:T(1,128)S(1)}, u32[]{:S(2)}, u32[]{:S(2)}) async-start(s32[2,1,12]{2,1,0:T(1,128)} %bitcast.4), calls=%async_computation | async-start | bytes 2048 | tf_op jit(solution)/shard_map/all_to_all | solution.py:57
  14.9 5.8 %collective-permute-start = (s32[1]{0:T(128)}, s32[1]{0:T(128)}, u32[]{:S(2)}, u32[]{:S(2)}) collective-permute-start(s32[1]{0:T(128)} %param.11), channel_id=1, source_target_pairs={{0,4},{4,8},{8,12},{12,0},{1,5},{5,9},{9,13},{13,1},{2,6},{6,10},{... | collective-permute-start | bytes 20 | tf_op jit(solution)/shard_map/while/body/eval_jaxpr/ppermute | solution.py:14
  20.8 5.3 %collective-permute-start.2 = (s32[1]{0:T(128)}, s32[1]{0:T(128)}, u32[]{:S(2)}, u32[]{:S(2)}) collective-permute-start(s32[1]{0:T(128)} %param.11), channel_id=1, source_target_pairs={{0,12},{4,0},{8,4},{12,8},{1,13},{5,1},{9,5},{13,9},{2,14},{6,2},{... | collective-permute-start | bytes 20 | tf_op jit(solution)/shard_map/while/body/eval_jaxpr/ppermute | solution.py:14
  26.1 5.9 %collective-permute-start.4 = (s32[1]{0:T(128)}, s32[1]{0:T(128)}, u32[]{:S(2)}, u32[]{:S(2)}) collective-permute-start(s32[1]{0:T(128)} %collective-permute-done), channel_id=1, source_target_pairs={{0,4},{4,8},{8,12},{12,0},{1,5},{5,9},{9,13},{13,1},{2,6},{6,10},{... | collective-permute-start | bytes 20 | tf_op jit(solution)/shard_map/ppermute | solution.py:14
  33.8 5.4 %collective-permute-start.5 = (s32[1,6]{1,0:T(1,128)S(1)}, s32[1,6]{1,0:T(1,128)S(1)}, u32[]{:S(2)}, u32[]{:S(2)}) collective-permute-start(s32[1,6]{1,0:T(1,128)S(1)} %collective-permute-done.1), channel_id=1, source_target_pairs={{0,4},{4,8},{8,12},{12,0},{1,5},{5,9},{9,13},{13,1},{2,6},{6,10},{... | collective-permute-start | bytes 80 | tf_op jit(solution)/shard_map/ppermute | solution.py:14
  43.3 7.0 %all-to-all-start.2 = ((bf16[2,12,120]{2,1,0:T(8,128)(2,1)}), bf16[2,12,120]{2,1,0:T(8,128)(2,1)S(1)}, u32[]{:S(2)}, u32[]{:S(2)}) async-start(bf16[2,12,120]{2,1,0:T(8,128)(2,1)} %broadcast_select_fusion.1), calls=%async_computation.2 | async-start | bytes 16384 | tf_op jit(solution)/shard_map/all_to_all | solution.py:69
  50.4 16.9 %all-to-all-start.1 = ((bf16[2,12,2,120,120]{4,3,2,1,0:T(8,128)(2,1)}), bf16[2,12,2,120,120]{4,3,2,1,0:T(8,128)(2,1)S(1)}, u32[]{:S(2)}, u32[]{:S(2)}) async-start(bf16[2,12,2,120,120]{4,3,2,1,0:T(8,128)(2,1)} %broadcast_select_fusion), calls=%async_computation.1 | async-start | bytes 2949120 | tf_op jit(solution)/shard_map/all_to_all | solution.py:68
  54.0 15.3 %copy-start.1 = (bf16[1,120,120]{2,1,0:T(8,128)(2,1)S(1)}, bf16[1,120,120]{2,1,0:T(8,128)(2,1)}, u32[]{:S(2)}) copy-start(bf16[1,120,120]{2,1,0:T(8,128)(2,1)} %param.10) | copy-start | bytes 86404
  55.2 18.4 %collective-permute-start.8 = (bf16[1,120,120]{2,1,0:T(8,128)(2,1)S(1)}, bf16[1,120,120]{2,1,0:T(8,128)(2,1)S(1)}, u32[]{:S(2)}, u32[]{:S(2)}) collective-permute-start(bf16[1,120,120]{2,1,0:T(8,128)(2,1)S(1)} %collective-permute-done.6), channel_id=1, source_target_pairs={{0,4},{4,8},{8,12},{12,0},{1,5},{5,9},{9,13},{13,1},{2,6},{6,10},{... | collective-permute-start | bytes 86408 | tf_op jit(solution)/shard_map/ppermute | solution.py:14
where the time goes:
time: 96.7 us; the launch traced here: 96.1 us
  waiting for transfers between devices  23.7 us (25%)
  starting transfers between devices  23.2 us (24%)
  matrix products  18.7 us (19%)
  local copies, waits for them, and re-layouts  12.5 us (13%)
  other arithmetic  7.97 us (8%)
  between operations  7.48 us (8%)
  blocking collectives  2.47 us (3%)
    ppermute x9, starting transfers between devices, passed_along(): return lax.ppermute(value, axis, pairs)  13.1 us
    dot_general x4, matrix products, finish(): return jnp.dot(power, weight_one, precision=lax.Precision.HIGHEST)  12.1 us
    all_to_all x1, waiting for transfers between devices, per_device(): lax.all_to_all(sent_blocks, 'trip', split_axis=0, concat_axis=0, tiled=True)  11.8 us
    ppermute x9, waiting for transfers between devices, passed_along(): return lax.ppermute(value, axis, pairs)  8.55 us
    dot_general x4, matrix products, finish(): jnp.dot(coeff_one, mixed_one, preferred_element_type=jnp.float32)  4.49 us
    all_to_all x1, starting transfers between devices, per_device(): lax.all_to_all(sent_blocks, 'trip', split_axis=0, concat_axis=0, tiled=True)  3.65 us
    all_to_all x1, waiting for transfers between devices, per_device(): lax.all_to_all(sent_levels, 'trip', split_axis=0, concat_axis=0, tiled=True)  3.32 us
    all_to_all x1, starting transfers between devices, per_device(): lax.all_to_all(sent_levels, 'trip', split_axis=0, concat_axis=0, tiled=True)  3.22 us
  transfers between devices with their start and end apart: 12, of which 4 were waited for; matrix products, arithmetic and copies ran while one was open for 20% of the time, Pallas kernels for 0%

commit v1 on v0

--- a/solution.py
+++ b/solution.py
@@ -1,8 +1,11 @@
+import functools
 import math
 
 import jax
 import jax.numpy as jnp
 from jax import lax
+from jax.experimental import pallas as pl
+from jax.experimental.pallas import tpu as pltpu
 from jax.sharding import PartitionSpec as P
 
 QGRID = 8
@@ -20,7 +23,7 @@
     )
 
 
-def per_device(
+def fetched_per_device(
     cubic_coupling_slices,
     leading_displacement_label,
     lattice_shift_pairs,
@@ -169,6 +172,388 @@
     return lax.psum_scatter(partial_sums, "rep", scatter_dimension=1, tiled=True)
 
 
+MESH = pl.DeviceIdType.MESH
+HALF_ROOT = math.sqrt(0.5)
+
+
+def pair_list(total_rows):
+    return [(a, b) for a in range(total_rows) for b in range(a + 1, total_rows)]
+
+
+def moved_kernel(
+    sizes,
+    phi_hbm,
+    label_hbm,
+    shift_hbm,
+    eig_hbm,
+    freq_hbm,
+    lookup_hbm,
+    trio_hbm,
+    heat_hbm,
+    out_ref,
+    phi,
+    label,
+    shift,
+    eig,
+    freq,
+    lookup,
+    trio,
+    heat,
+    mixer,
+    hidden,
+    mixed,
+    result,
+    local_got,
+    far_got,
+    load_sem,
+    row_send,
+    row_recv,
+    trio_send,
+    trio_recv,
+    back_send,
+    back_recv,
+):
+    loops, reps, rows_dev, width, trip_dev, q_held = sizes
+    half = trip_dev // reps
+    total_rows = rows_dev * loops
+    columns = width // reps
+    here_loop = lax.axis_index("loop")
+    here_trip = lax.axis_index("trip")
+    here_rep = lax.axis_index("rep")
+    other_trip = 1 - here_trip
+
+    loads = [
+        pltpu.make_async_copy(src, dst, load_sem.at[n])
+        for n, (src, dst) in enumerate(
+            [
+                (trio_hbm, trio.at[0]),
+                (lookup_hbm, lookup),
+                (heat_hbm, heat.at[0]),
+                (label_hbm, label.at[0]),
+                (shift_hbm, shift.at[0]),
+                (freq_hbm, freq),
+                (eig_hbm, eig),
+                (phi_hbm, phi.at[0]),
+            ]
+        )
+    ]
+    for load in loads:
+        load.start()
+
+    barrier = pltpu.get_barrier_semaphore()
+    ups = [lax.rem(here_loop + step, loops) for step in range(1, loops)]
+    reps_away = [lax.rem(here_rep + step, reps) for step in range(1, reps)]
+    for up in ups:
+        pl.semaphore_signal(barrier, inc=1, device_id={"loop": up}, device_id_type=MESH)
+    for rep in reps_away:
+        pl.semaphore_signal(barrier, inc=1, device_id={"rep": rep}, device_id_type=MESH)
+    for rep in [here_rep] + reps_away:
+        pl.semaphore_signal(
+            barrier, inc=1, device_id={"trip": other_trip, "rep": rep}, device_id_type=MESH
+        )
+    pl.semaphore_wait(barrier, (loops - 1) + (reps - 1) + reps)
+
+    trio_copies = []
+    for n, (src, dst) in enumerate([(trio_hbm, trio.at[1]), (heat_hbm, heat.at[1])]):
+        trio_copies.append(
+            pltpu.make_async_remote_copy(
+                src_ref=src,
+                dst_ref=dst,
+                send_sem=trio_send.at[n],
+                recv_sem=trio_recv.at[n],
+                device_id={"trip": other_trip},
+                device_id_type=MESH,
+            )
+        )
+    row_copies = []
+    for step in range(1, loops):
+        for n, (src, dst) in enumerate(
+            [
+                (label_hbm, label.at[step]),
+                (shift_hbm, shift.at[step]),
+                (phi_hbm, phi.at[step]),
+            ]
+        ):
+            row_copies.append(
+                pltpu.make_async_remote_copy(
+                    src_ref=src,
+                    dst_ref=dst,
+                    send_sem=row_send.at[step, n],
+                    recv_sem=row_recv.at[step, n],
+                    device_id={"loop": ups[step - 1]},
+                    device_id_type=MESH,
+                )
+            )
+    for copy in trio_copies + row_copies:
+        copy.start()
+
+    hidden[...] = jnp.zeros_like(hidden)
+    mixer[...] = jnp.zeros_like(mixer)
+    for load in loads:
+        load.wait()
+    for copy in trio_copies:
+        copy.wait()
+
+    def turned(block):
+        return jnp.swapaxes(block.astype(jnp.float32), 0, 1).astype(jnp.bfloat16)
+
+    jobs = []
+    for side in range(2):
+        for item in range(half):
+            row = here_rep * half + item
+            points = [trio[side, row, n] for n in range(3)]
+            slots = [lax.rem(lookup[point], q_held) for point in points]
+            kelvin = 0.5 * (heat[side, row].astype(jnp.float32) + 1.0)
+            jobs.append((points, slots, kelvin))
+
+    for n, (points, slots, kelvin) in enumerate(jobs):
+        back_re = turned(eig[slots[1], 0])
+        back_im = turned(eig[slots[1], 1])
+        mixer[n, 0:width, 0:width] = back_re
+        mixer[n, 0:width, 128 : 128 + width] = -back_im
+        mixer[n, 128 : 128 + width, 0:width] = back_im
+        mixer[n, 128 : 128 + width, 128 : 128 + width] = back_re
+
+    for step in range(loops):
+        if step:
+            for copy in row_copies[3 * (step - 1) : 3 * step]:
+                copy.wait_recv()
+        for inner in range(rows_dev):
+            block = phi[step, inner]
+            at = (step * rows_dev + inner) * 128
+            for n, (points, slots, kelvin) in enumerate(jobs):
+                for part in range(2):
+                    hidden[n, part * 128 : part * 128 + width, at : at + width] = jnp.dot(
+                        block, eig[slots[2], part], preferred_element_type=jnp.float32
+                    ).astype(jnp.bfloat16)
+
+    job_count = len(jobs)
+    lanes = lax.broadcasted_iota(jnp.int32, (8, q_held), 1)
+    ranks = lax.broadcasted_iota(jnp.int32, (8, q_held), 0)
+    picks = []
+    for which in range(3):
+        wanted = jnp.zeros((8, q_held), jnp.int32)
+        for n, (points, slots, kelvin) in enumerate(jobs):
+            wanted = jnp.where(ranks == n, slots[which], wanted)
+        hot = jnp.where(wanted == lanes, 1.0, 0.0).astype(jnp.bfloat16)
+        picks.append(jnp.dot(hot, freq[...], preferred_element_type=jnp.float32))
+    temper_ranks = lax.broadcasted_iota(jnp.int32, (8, width), 0)
+    temper = jnp.ones((8, width), jnp.float32)
+    for n, (points, slots, kelvin) in enumerate(jobs):
+        temper = jnp.where(temper_ranks == n, kelvin, temper)
+    first_level, second_level, third_level = [
+        jnp.where(temper_ranks < job_count, pick, 1.0) for pick in picks
+    ]
+    second_scale = 1.0 / second_level
+    third_scale = 1.0 / third_level
+    second_part = (1.0 + 1.0 / (jnp.exp(second_level / temper) - 1.0)) * second_scale
+    third_part = third_scale / (jnp.exp(third_level / temper) - 1.0)
+    second_scale_col = jnp.swapaxes(second_scale, 0, 1)
+    second_part_col = jnp.swapaxes(second_part, 0, 1)
+    out_scale = (1.0 / (8.0 * width * total_rows)) / first_level
+
+    pairs = pair_list(total_rows)
+    padded_rows = -(-total_rows // 8) * 8
+    row_ids = lax.broadcasted_iota(jnp.int32, (padded_rows, width), 0)
+    col_ids = lax.broadcasted_iota(jnp.int32, (padded_rows, width), 1)
+    named = jnp.zeros((padded_rows, width), jnp.int32)
+    for s in range(total_rows):
+        named = jnp.where(row_ids == s, label[s // rows_dev, s % rows_dev], named)
+    hot_label = jnp.where(named == col_ids, 1.0, 0.0).astype(jnp.bfloat16)
+
+    for n, (points, slots, kelvin) in enumerate(jobs):
+        mixed[...] = jnp.dot(mixer[n], hidden[n], preferred_element_type=jnp.float32)
+        sums = [None] * (total_rows + 2 * len(pairs))
+
+        def put(index, value):
+            sums[index] = value if sums[index] is None else sums[index] + value
+
+        for top in range(0, width, 8):
+            weight = (
+                second_part_col[top : top + 8, n : n + 1] * third_scale[n : n + 1]
+                + second_scale_col[top : top + 8, n : n + 1] * third_part[n : n + 1]
+            )
+            re = [
+                mixed[top : top + 8, s * 128 : s * 128 + width] for s in range(total_rows)
+            ]
+            im = [
+                mixed[128 + top : 136 + top, s * 128 : s * 128 + width]
+                for s in range(total_rows)
+            ]
+            wre = [weight * v for v in re]
+            wim = [weight * v for v in im]
+            for s in range(total_rows):
+                put(s, wre[s] * re[s] + wim[s] * im[s])
+            for m, (a, b) in enumerate(pairs):
+                put(total_rows + 2 * m, wre[a] * re[b] + wim[a] * im[b])
+                put(total_rows + 2 * m + 1, wim[a] * re[b] - wre[a] * im[b])
+
+        turns = jnp.zeros((padded_rows, width), jnp.int32)
+        grids = []
+        for point in points[1:]:
+            grids += [
+                lax.rem(point, QGRID),
+                lax.rem(lax.div(point, QGRID), QGRID),
+                lax.rem(lax.div(point, QGRID * QGRID), QGRID),
+            ]
+        for s in range(total_rows):
+            turn = 0
+            for m in range(6):
+                turn = turn + grids[m] * (shift[s // rows_dev, s % rows_dev, m] - 1)
+            turns = jnp.where(row_ids == s, turn, turns)
+        turns = jnp.bitwise_and(turns, QGRID - 1)
+
+        def cosine_of(k):
+            k = jnp.bitwise_and(k, QGRID - 1)
+            flipped = jnp.minimum(k, QGRID - k)
+            return jnp.where(
+                flipped == 0,
+                1.0,
+                jnp.where(
+                    flipped == 1,
+                    HALF_ROOT,
+                    jnp.where(flipped == 2, 0.0, jnp.where(flipped == 3, -HALF_ROOT, -1.0)),
+                ),
+            ).astype(jnp.float32)
+
+        cosine = cosine_of(turns)
+        sine = cosine_of(turns + (QGRID - QGRID // 4))
+        picked_re = jnp.dot(hot_label, eig[slots[0], 0], preferred_element_type=jnp.float32)
+        picked_im = jnp.dot(hot_label, eig[slots[0], 1], preferred_element_type=jnp.float32)
+        coef_re = (
+            (picked_re * cosine - picked_im * sine).astype(jnp.bfloat16).astype(jnp.float32)
+        )
+        coef_im = (
+            (picked_re * sine + picked_im * cosine).astype(jnp.bfloat16).astype(jnp.float32)
+        )
+        total = jnp.zeros((1, width), jnp.float32)
+        for index, value in enumerate(sums):
+            scalar = jnp.sum(jnp.sum(value, axis=0, keepdims=True), axis=1, keepdims=True)
+            if index < total_rows:
+                a = slice(index, index + 1)
+                term = coef_re[a] * coef_re[a] + coef_im[a] * coef_im[a]
+            else:
+                a, b = pairs[(index - total_rows) // 2]
+                a, b = slice(a, a + 1), slice(b, b + 1)
+                if (index - total_rows) % 2 == 0:
+                    term = 2.0 * (coef_re[a] * coef_re[b] + coef_im[a] * coef_im[b])
+                else:
+                    term = -2.0 * (coef_im[a] * coef_re[b] - coef_re[a] * coef_im[b])
+            total = total + scalar * term
+        side, item = n // half, n % half
+        result[side, item : item + 1, 0:width] = total * out_scale[n : n + 1]
+
+    back = []
+    for m, step in enumerate(range(1, reps)):
+        back.append(
+            pltpu.make_async_remote_copy(
+                src_ref=result.at[0],
+                dst_ref=local_got.at[m],
+                send_sem=back_send.at[m],
+                recv_sem=back_recv.at[m],
+                device_id={"rep": reps_away[m]},
+                device_id_type=MESH,
+            )
+        )
+    for step, rep in enumerate([here_rep] + reps_away):
+        back.append(
+            pltpu.make_async_remote_copy(
+                src_ref=result.at[1],
+                dst_ref=far_got.at[step],
+                send_sem=back_send.at[reps - 1 + step],
+                recv_sem=back_recv.at[reps - 1 + step],
+                device_id={"trip": other_trip, "rep": rep},
+                device_id_type=MESH,
+            )
+        )
+    for copy in back:
+        copy.start()
+    for copy in back:
+        copy.wait()
+    for copy in row_copies:
+        copy.wait_send()
+
+    near = [result[0, 0:half]] + [local_got[m, 0:half] for m in range(reps - 1)]
+    far = [far_got[step, 0:half] for step in range(reps)]
+    ordered = []
+    for rep in range(reps):
+        near_rep, far_rep = near[0], far[0]
+        for step in range(1, reps):
+            came = lax.rem(here_rep + reps - step, reps) == rep
+            near_rep = jnp.where(came, near[step], near_rep)
+            far_rep = jnp.where(came, far[step], far_rep)
+        for item in range(half):
+            point = trio[0, rep * half + item, 0]
+            held_here = lax.div(lookup[point], q_held) == here_trip
+            ordered.append(
+                jnp.where(held_here, near_rep[item : item + 1], far_rep[item : item + 1])
+            )
+    whole = jnp.concatenate(ordered, axis=0)
+    shifted = whole[:, 0:columns]
+    for rep in range(1, reps):
+        shifted = jnp.where(
+            here_rep == rep, whole[:, rep * columns : (rep + 1) * columns], shifted
+        )
+    out_ref[...] = shifted
+
+
+def moved_per_device(phi, label, shift, eig, freq, lookup, trio, heat):
+    loops, reps = lax.axis_size("loop"), lax.axis_size("rep")
+    rows_dev, width = phi.shape[:2]
+    trip_dev = trio.shape[0]
+    q_held = eig.shape[0]
+    total_rows = rows_dev * loops
+    half = trip_dev // reps
+    jobs = 2 * half
+    sizes = (loops, reps, rows_dev, width, trip_dev, q_held)
+    dma = pltpu.SemaphoreType.DMA
+    half_pad = -(-half // 8) * 8
+    return pl.pallas_call(
+        functools.partial(moved_kernel, sizes),
+        out_shape=jax.ShapeDtypeStruct((trip_dev, width // reps), jnp.float32),
+        in_specs=[pl.BlockSpec(memory_space=pl.ANY)] * 8,
+        out_specs=pl.BlockSpec(memory_space=pltpu.VMEM),
+        scratch_shapes=[
+            pltpu.VMEM((loops,) + phi.shape, phi.dtype),
+            pltpu.SMEM((loops,) + label.shape, jnp.int32),
+            pltpu.SMEM((loops,) + shift.shape, jnp.int32),
+            pltpu.VMEM(eig.shape, eig.dtype),
+            pltpu.VMEM(freq.shape, freq.dtype),
+            pltpu.SMEM(lookup.shape, jnp.int32),
+            pltpu.SMEM((2,) + trio.shape, jnp.int32),
+            pltpu.SMEM((2,) + heat.shape, jnp.int32),
+            pltpu.VMEM((jobs, 256, 256), jnp.bfloat16),
+            pltpu.VMEM((jobs, 256, 128 * total_rows), jnp.bfloat16),
+            pltpu.VMEM((256, 128 * total_rows), jnp.float32),
+            pltpu.VMEM((2, half_pad, 128), jnp.float32),
+            pltpu.VMEM((reps - 1, half_pad, 128), jnp.float32),
+            pltpu.VMEM((reps, half_pad, 128), jnp.float32),
+            dma((8,)),
+            dma((loops, 3)),
+            dma((loops, 3)),
+            dma((2,)),
+            dma((2,)),
+            dma((2 * reps - 1,)),
+            dma((2 * reps - 1,)),
+        ],
+        compiler_params=pltpu.CompilerParams(collective_id=0, has_side_effects=True),
+    )(phi, label, shift, eig, freq, lookup, trio, heat)
+
+
+def per_device(phi, label, shift, eig, freq, lookup, trio, heat):
+    reps = lax.axis_size("rep")
+    moved = (
+        lax.axis_size("trip") == 2
+        and lax.axis_size("loop") * phi.shape[0] <= 8
+        and trio.shape[0] % reps == 0
+        and reps > 1
+        and phi.shape[1] <= 128
+        and phi.shape[1] % 8 == 0
+    )
+    call = moved_per_device if moved else fetched_per_device
+    return call(phi, label, shift, eig, freq, lookup, trio, heat)
+
+
 def solution(mesh):
     in_specs = (
         P(("dom", "loop"), None, None),

time: 96.7 us -> 16.7 us (0.17)
  waiting for transfers between devices: 23.7 us -> 0 us
  starting transfers between devices: 23.2 us -> 0 us
  matrix products: 18.7 us -> 0 us
  Pallas kernels: 0 us -> 14.6 us
  local copies, waits for them, and re-layouts: 12.5 us -> 1.26 us
  other arithmetic: 7.97 us -> 0 us
  between operations: 7.48 us -> 0.66 us
  blocking collectives: 2.47 us -> 0 us
    dot_general x16 -> x0, matrix products: 18.7 us -> none  [the longest x4 12.1 us: finish(): return jnp.dot(power, weight_one, precision=lax.Precision.HIGHEST)]
    all_to_all x3 -> x0, waiting for transfers between devices: 15.1 us -> none  [the longest x1 11.8 us: per_device(): lax.all_to_all(sent_blocks, 'trip', split_axis=0, concat_axis=0, tiled=True)]
    pallas_call x0 -> x1, Pallas kernels: none -> 14.6 us  [moved_per_device(): pl.pallas_call(functools.partial(moved_kernel, sizes), out_shape=jax.Shap...]
    ppermute x9 -> x0, starting transfers between devices: 13.1 us -> none  [passed_along(): return lax.ppermute(value, axis, pairs)]
    all_to_all x3 -> x0, starting transfers between devices: 10.1 us -> none  [the longest x1 3.65 us: per_device(): lax.all_to_all(sent_blocks, 'trip', split_axis=0, concat_axis=0, tiled=True)]
    ppermute x9 -> x0, waiting for transfers between devices: 8.55 us -> none  [passed_along(): return lax.ppermute(value, axis, pairs)]
    gather x5 -> x0, local copies, waits for them, and re-layouts: 3.36 us -> none  [the longest x2 1.28 us: per_device(): mode_pulsations[chosen]]
    select_n x5 -> x0, other arithmetic: 3.02 us -> none  [the longest x1 1.3 us: per_device(): jnp.where(usable[:, :, None, None, None], polarization_vectors[chosen], j...]
  transfers between devices with their start and end apart: 12 -> 0, of which waited for: 4 -> 0; matrix products, arithmetic and copies ran while one was open for 20% -> 0% of each run, Pallas kernels for 0% -> 0%
where the time goes in v1:
time: 16.7 us; the launch traced here: 16.5 us
  Pallas kernels  14.6 us (87%)
  local copies, waits for them, and re-layouts  1.26 us (8%)
  between operations  0.66 us (4%)
    pallas_call x1, Pallas kernels, moved_per_device(): pl.pallas_call(functools.partial(moved_kernel, sizes), out_shape=jax.Shap...  14.6 us
    unnamed x1, local copies, waits for them, and re-layouts  1.26 us

profile of v1, /device:TPU:0, one launch (start us, length us, event | category | flops | bytes accessed | tf_op | source)
XLA Modules:
  0.0 16.5 jit_solution(14198271642983097479)
XLA Ops:
  0.7 14.6 %shard_map.82 = f32[4,60]{1,0:T(4,128)} custom-call(bf16[1,120,120]{2,1,0:T(8,128)(2,1)} %phi_hbm.1, s32[1]{0:T(128)S(6)} %copy.10.label_hbm, s32[1,6]{1,0:T(1,128)} %shift_hbm.1, bf16[16,2,120,120]{3,2,1,0:T(8,128)(2,1)} %eig_hbm.1, bf16[16,120]{1,0:T(8,128)(2,1)} %freq_hbm.1, s32[32]{0:T(128)} %lookup_hbm.1, s32[4,3]{1,0:T(4,128)} %trio_hbm.1, s32[4]{0:T(128)} %heat_hbm.1), custom_call_target="tpu_custom_call" | custom-call | tf_op jit(solution)/shard_map/pallas_call | solution.py:511
  15.3 1.3 %copy.11 = f32[4,60]{1,0:T(4,128)} copy(f32[4,60]{1,0:T(4,128)} %shard_map.82) | data formatting | bytes 1920

commit v2 on v1

--- a/solution.py
+++ b/solution.py
@@ -177,7 +177,7 @@
 
 
 def pair_list(total_rows):
-    return [(a, b) for a in range(total_rows) for b in range(a + 1, total_rows)]
+    return [(a, a + gap) for gap in range(1, total_rows) for a in range(total_rows - gap)]
 
 
 def moved_kernel(
@@ -237,9 +237,6 @@
             ]
         )
     ]
-    for load in loads:
-        load.start()
-
     barrier = pltpu.get_barrier_semaphore()
     ups = [lax.rem(here_loop + step, loops) for step in range(1, loops)]
     reps_away = [lax.rem(here_rep + step, reps) for step in range(1, reps)]
@@ -251,6 +248,10 @@
         pl.semaphore_signal(
             barrier, inc=1, device_id={"trip": other_trip, "rep": rep}, device_id_type=MESH
         )
+
+    for load in loads:
+        load.start()
+
     pl.semaphore_wait(barrier, (loops - 1) + (reps - 1) + reps)
 
     trio_copies = []
@@ -291,22 +292,18 @@
     mixer[...] = jnp.zeros_like(mixer)
     for load in loads:
         load.wait()
-    for copy in trio_copies:
-        copy.wait()
 
     def turned(block):
         return jnp.swapaxes(block.astype(jnp.float32), 0, 1).astype(jnp.bfloat16)
 
-    jobs = []
-    for side in range(2):
-        for item in range(half):
-            row = here_rep * half + item
-            points = [trio[side, row, n] for n in range(3)]
-            slots = [lax.rem(lookup[point], q_held) for point in points]
-            kelvin = 0.5 * (heat[side, row].astype(jnp.float32) + 1.0)
-            jobs.append((points, slots, kelvin))
-
-    for n, (points, slots, kelvin) in enumerate(jobs):
+    def job_of(side, item):
+        row = here_rep * half + item
+        points = [trio[side, row, n] for n in range(3)]
+        slots = [lax.rem(lookup[point], q_held) for point in points]
+        kelvin = 0.5 * (heat[side, row].astype(jnp.float32) + 1.0)
+        return points, slots, kelvin
+
+    def set_mixer(n, slots):
         back_re = turned(eig[slots[1], 0])
         back_im = turned(eig[slots[1], 1])
         mixer[n, 0:width, 0:width] = back_re
@@ -314,18 +311,32 @@
         mixer[n, 128 : 128 + width, 0:width] = back_im
         mixer[n, 128 : 128 + width, 128 : 128 + width] = back_re
 
-    for step in range(loops):
-        if step:
-            for copy in row_copies[3 * (step - 1) : 3 * step]:
-                copy.wait_recv()
+    def set_hidden(n, slots, step):
         for inner in range(rows_dev):
-            block = phi[step, inner]
             at = (step * rows_dev + inner) * 128
-            for n, (points, slots, kelvin) in enumerate(jobs):
-                for part in range(2):
-                    hidden[n, part * 128 : part * 128 + width, at : at + width] = jnp.dot(
-                        block, eig[slots[2], part], preferred_element_type=jnp.float32
-                    ).astype(jnp.bfloat16)
+            for part in range(2):
+                hidden[n, part * 128 : part * 128 + width, at : at + width] = jnp.dot(
+                    phi[step, inner], eig[slots[2], part], preferred_element_type=jnp.float32
+                ).astype(jnp.bfloat16)
+
+    def set_mixed(n, steps):
+        low, high = steps[0] * rows_dev * 128, (steps[-1] + 1) * rows_dev * 128
+        mixed[n, :, low:high] = jnp.dot(
+            mixer[n], hidden[n, :, low:high], preferred_element_type=jnp.float32
+        )
+
+    jobs = [job_of(0, item) for item in range(half)]
+    for n, (points, slots, kelvin) in enumerate(jobs):
+        set_mixer(n, slots)
+        set_hidden(n, slots, 0)
+
+    for copy in trio_copies:
+        copy.wait_recv()
+    jobs += [job_of(1, item) for item in range(half)]
+    for n, (points, slots, kelvin) in enumerate(jobs):
+        if n >= half:
+            set_mixer(n, slots)
+            set_hidden(n, slots, 0)
 
     job_count = len(jobs)
     lanes = lax.broadcasted_iota(jnp.int32, (8, q_held), 1)
@@ -352,6 +363,17 @@
     second_part_col = jnp.swapaxes(second_part, 0, 1)
     out_scale = (1.0 / (8.0 * width * total_rows)) / first_level
 
+    for step in range(1, loops):
+        for copy in row_copies[3 * (step - 1) : 3 * step]:
+            copy.wait_recv()
+        for n, (points, slots, kelvin) in enumerate(jobs):
+            set_hidden(n, slots, step)
+        if step == loops // 2 - 1:
+            for n in range(len(jobs)):
+                set_mixed(n, range(loops // 2))
+    for n in range(len(jobs)):
+        set_mixed(n, range(loops // 2, loops))
+
     pairs = pair_list(total_rows)
     padded_rows = -(-total_rows // 8) * 8
     row_ids = lax.broadcasted_iota(jnp.int32, (padded_rows, width), 0)
@@ -362,7 +384,6 @@
     hot_label = jnp.where(named == col_ids, 1.0, 0.0).astype(jnp.bfloat16)
 
     for n, (points, slots, kelvin) in enumerate(jobs):
-        mixed[...] = jnp.dot(mixer[n], hidden[n], preferred_element_type=jnp.float32)
         sums = [None] * (total_rows + 2 * len(pairs))
 
         def put(index, value):
@@ -374,10 +395,10 @@
                 + second_scale_col[top : top + 8, n : n + 1] * third_part[n : n + 1]
             )
             re = [
-                mixed[top : top + 8, s * 128 : s * 128 + width] for s in range(total_rows)
+                mixed[n, top : top + 8, s * 128 : s * 128 + width] for s in range(total_rows)
             ]
             im = [
-                mixed[128 + top : 136 + top, s * 128 : s * 128 + width]
+                mixed[n, 128 + top : 136 + top, s * 128 : s * 128 + width]
                 for s in range(total_rows)
             ]
             wre = [weight * v for v in re]
@@ -385,8 +406,8 @@
             for s in range(total_rows):
                 put(s, wre[s] * re[s] + wim[s] * im[s])
             for m, (a, b) in enumerate(pairs):
-                put(total_rows + 2 * m, wre[a] * re[b] + wim[a] * im[b])
-                put(total_rows + 2 * m + 1, wim[a] * re[b] - wre[a] * im[b])
+                put(total_rows + m, wre[a] * re[b] + wim[a] * im[b])
+                put(total_rows + len(pairs) + m, wim[a] * re[b] - wre[a] * im[b])
 
         turns = jnp.zeros((padded_rows, width), jnp.int32)
         grids = []
@@ -426,20 +447,16 @@
         coef_im = (
             (picked_re * sine + picked_im * cosine).astype(jnp.bfloat16).astype(jnp.float32)
         )
-        total = jnp.zeros((1, width), jnp.float32)
-        for index, value in enumerate(sums):
-            scalar = jnp.sum(jnp.sum(value, axis=0, keepdims=True), axis=1, keepdims=True)
-            if index < total_rows:
-                a = slice(index, index + 1)
-                term = coef_re[a] * coef_re[a] + coef_im[a] * coef_im[a]
-            else:
-                a, b = pairs[(index - total_rows) // 2]
-                a, b = slice(a, a + 1), slice(b, b + 1)
-                if (index - total_rows) % 2 == 0:
-                    term = 2.0 * (coef_re[a] * coef_re[b] + coef_im[a] * coef_im[b])
-                else:
-                    term = -2.0 * (coef_im[a] * coef_re[b] - coef_re[a] * coef_im[b])
-            total = total + scalar * term
+        diag = coef_re[0:total_rows] ** 2 + coef_im[0:total_rows] ** 2
+        cross_re, cross_im = [], []
+        for gap in range(1, total_rows):
+            a, b = slice(0, total_rows - gap), slice(gap, total_rows)
+            cross_re.append(2.0 * (coef_re[a] * coef_re[b] + coef_im[a] * coef_im[b]))
+            cross_im.append(2.0 * (coef_re[a] * coef_im[b] - coef_im[a] * coef_re[b]))
+        terms = jnp.concatenate([diag] + cross_re + cross_im, axis=0)
+        grams = jnp.concatenate([jnp.sum(v, axis=0, keepdims=True) for v in sums], axis=0)
+        grams = jnp.sum(grams, axis=1, keepdims=True)
+        total = jnp.sum(grams * terms, axis=0, keepdims=True)
         side, item = n // half, n % half
         result[side, item : item + 1, 0:width] = total * out_scale[n : n + 1]
 
@@ -470,7 +487,7 @@
         copy.start()
     for copy in back:
         copy.wait()
-    for copy in row_copies:
+    for copy in trio_copies + row_copies:
         copy.wait_send()
 
     near = [result[0, 0:half]] + [local_got[m, 0:half] for m in range(reps - 1)]
@@ -511,7 +528,7 @@
     return pl.pallas_call(
         functools.partial(moved_kernel, sizes),
         out_shape=jax.ShapeDtypeStruct((trip_dev, width // reps), jnp.float32),
-        in_specs=[pl.BlockSpec(memory_space=pl.ANY)] * 8,
+        in_specs=[pl.BlockSpec(memory_space=pltpu.HBM)] * 8,
         out_specs=pl.BlockSpec(memory_space=pltpu.VMEM),
         scratch_shapes=[
             pltpu.VMEM((loops,) + phi.shape, phi.dtype),
@@ -524,7 +541,7 @@
             pltpu.SMEM((2,) + heat.shape, jnp.int32),
             pltpu.VMEM((jobs, 256, 256), jnp.bfloat16),
             pltpu.VMEM((jobs, 256, 128 * total_rows), jnp.bfloat16),
-            pltpu.VMEM((256, 128 * total_rows), jnp.float32),
+            pltpu.VMEM((jobs, 256, 128 * total_rows), jnp.float32),
             pltpu.VMEM((2, half_pad, 128), jnp.float32),
             pltpu.VMEM((reps - 1, half_pad, 128), jnp.float32),
             pltpu.VMEM((reps, half_pad, 128), jnp.float32),
@@ -544,6 +561,7 @@
     reps = lax.axis_size("rep")
     moved = (
         lax.axis_size("trip") == 2
+        and lax.axis_size("loop") >= 4
         and lax.axis_size("loop") * phi.shape[0] <= 8
         and trio.shape[0] % reps == 0
         and reps > 1

time: 16.7 us -> 16.5 us (0.988)
  Pallas kernels: 14.6 us -> 14.4 us
    pallas_call x1, Pallas kernels: 14.6 us -> 14.4 us  [moved_per_device(): pl.pallas_call(functools.partial(moved_kernel, sizes), out_shape=jax.Shap...]
where the time goes in v2:
time: 16.5 us; the launch traced here: 16.3 us
  Pallas kernels  14.4 us (87%)
  local copies, waits for them, and re-layouts  1.26 us (8%)
  between operations  0.66 us (4%)
    pallas_call x1, Pallas kernels, moved_per_device(): pl.pallas_call(functools.partial(moved_kernel, sizes), out_shape=jax.Shap...  14.4 us
    unnamed x1, local copies, waits for them, and re-layouts  1.26 us

profile of v2, /device:TPU:0, one launch (start us, length us, event | category | flops | bytes accessed | tf_op | source)
XLA Modules:
  0.0 16.3 jit_solution(15037984158184661274)
XLA Ops:
  0.7 14.4 %shard_map.82 = f32[4,60]{1,0:T(4,128)} custom-call(bf16[1,120,120]{2,1,0:T(8,128)(2,1)} %phi_hbm.1, s32[1]{0:T(128)S(6)} %copy.10.label_hbm, s32[1,6]{1,0:T(1,128)} %shift_hbm.1, bf16[16,2,120,120]{3,2,1,0:T(8,128)(2,1)} %eig_hbm.1, bf16[16,120]{1,0:T(8,128)(2,1)} %freq_hbm.1, s32[32]{0:T(128)} %lookup_hbm.1, s32[4,3]{1,0:T(4,128)} %trio_hbm.1, s32[4]{0:T(128)} %heat_hbm.1), custom_call_target="tpu_custom_call" | custom-call | tf_op jit(solution)/shard_map/pallas_call | solution.py:528
  15.1 1.3 %copy.11 = f32[4,60]{1,0:T(4,128)} copy(f32[4,60]{1,0:T(4,128)} %shard_map.82) | data formatting | bytes 1920

commit v3 on v2

--- a/solution.py
+++ b/solution.py
@@ -383,7 +383,7 @@
         named = jnp.where(row_ids == s, label[s // rows_dev, s % rows_dev], named)
     hot_label = jnp.where(named == col_ids, 1.0, 0.0).astype(jnp.bfloat16)
 
-    for n, (points, slots, kelvin) in enumerate(jobs):
+    def finish(n, points, slots):
         sums = [None] * (total_rows + 2 * len(pairs))
 
         def put(index, value):
@@ -460,7 +460,24 @@
         side, item = n // half, n % half
         result[side, item : item + 1, 0:width] = total * out_scale[n : n + 1]
 
+    for n in range(half, 2 * half):
+        finish(n, jobs[n][0], jobs[n][1])
     back = []
+    for step, rep in enumerate([here_rep] + reps_away):
+        back.append(
+            pltpu.make_async_remote_copy(
+                src_ref=result.at[1],
+                dst_ref=far_got.at[step],
+                send_sem=back_send.at[reps - 1 + step],
+                recv_sem=back_recv.at[reps - 1 + step],
+                device_id={"trip": other_trip, "rep": rep},
+                device_id_type=MESH,
+            )
+        )
+    for copy in back:
+        copy.start()
+    for n in range(half):
+        finish(n, jobs[n][0], jobs[n][1])
     for m, step in enumerate(range(1, reps)):
         back.append(
             pltpu.make_async_remote_copy(
@@ -472,18 +489,7 @@
                 device_id_type=MESH,
             )
         )
-    for step, rep in enumerate([here_rep] + reps_away):
-        back.append(
-            pltpu.make_async_remote_copy(
-                src_ref=result.at[1],
-                dst_ref=far_got.at[step],
-                send_sem=back_send.at[reps - 1 + step],
-                recv_sem=back_recv.at[reps - 1 + step],
-                device_id={"trip": other_trip, "rep": rep},
-                device_id_type=MESH,
-            )
-        )
-    for copy in back:
+    for copy in back[reps:]:
         copy.start()
     for copy in back:
         copy.wait()

time: 16.5 us -> 16.2 us (0.982)
  Pallas kernels: 14.4 us -> 14.1 us
    pallas_call x1, Pallas kernels: 14.4 us -> 14.1 us  [moved_per_device(): pl.pallas_call(functools.partial(moved_kernel, sizes), out_shape=jax.Shap...]
where the time goes in v3:
time: 16.2 us; the launch traced here: 16 us
  Pallas kernels  14.1 us (87%)
  local copies, waits for them, and re-layouts  1.26 us (8%)
  between operations  0.66 us (4%)
    pallas_call x1, Pallas kernels, moved_per_device(): pl.pallas_call(functools.partial(moved_kernel, sizes), out_shape=jax.Shap...  14.1 us
    unnamed x1, local copies, waits for them, and re-layouts  1.26 us

profile of v3, /device:TPU:0, one launch (start us, length us, event | category | flops | bytes accessed | tf_op | source)
XLA Modules:
  0.0 16.0 jit_solution(2934959502546020075)
XLA Ops:
  0.7 14.1 %shard_map.82 = f32[4,60]{1,0:T(4,128)} custom-call(bf16[1,120,120]{2,1,0:T(8,128)(2,1)} %phi_hbm.1, s32[1]{0:T(128)S(6)} %copy.10.label_hbm, s32[1,6]{1,0:T(1,128)} %shift_hbm.1, bf16[16,2,120,120]{3,2,1,0:T(8,128)(2,1)} %eig_hbm.1, bf16[16,120]{1,0:T(8,128)(2,1)} %freq_hbm.1, s32[32]{0:T(128)} %lookup_hbm.1, s32[4,3]{1,0:T(4,128)} %trio_hbm.1, s32[4]{0:T(128)} %heat_hbm.1), custom_call_target="tpu_custom_call" | custom-call | tf_op jit(solution)/shard_map/pallas_call | solution.py:534
  14.7 1.3 %copy.11 = f32[4,60]{1,0:T(4,128)} copy(f32[4,60]{1,0:T(4,128)} %shard_map.82) | data formatting | bytes 1920
